TPU v7x, 32 devices: a whole 2x2x4 slice. The times are simulated.
32 devices in a mesh: mem: 4 (over x, core), row: 4 (over z), col: 2 (over y).
Axes of the slice: x: 2, y: 2, z: 4, core: 2. Of those that a mesh axis runs over, the one named last changes fastest.
Arguments:
- fields: bfloat16 [16, 16, 64, 256], P('mem', 'row', 'col'), may hold values from -6 to 6
- norm_gain: float32 [256], replicated, may hold values from 0.5 to 1.5
- w_query: bfloat16 [256, 256], replicated, may hold values from -11 to 11
- w_key: bfloat16 [256, 256], replicated, may hold values from -6 to 6
- w_value: bfloat16 [256, 256], replicated, may hold values from -0.375 to 0.375
- w_out: bfloat16 [256, 256], replicated, may hold values from -0.375 to 0.375
- mix_kernel: float32 [3, 3, 256], replicated, may hold values from -1.5 to 1.5
- cotangent: bfloat16 [16, 16, 64, 256], P('mem', 'row', 'col'), may hold values from -6 to 6
Outputs:
- grad_fields: bfloat16 [16, 16, 64, 256], P('mem', 'row', 'col')
- grad_gain: float32 [256], replicated
- grad_query: float32 [256, 256], replicated
- grad_key: float32 [256, 256], replicated
- grad_value: float32 [256, 256], replicated
- grad_out: float32 [256, 256], replicated
- grad_kernel: float32 [3, 3, 256], replicated
All inputs are finite; a program needn't handle non-finite values.
Results may differ from a plain program's by a relative error of at most 0.015.
The roundings to bfloat16 on the way count: a program that leaves them out, or rounds other values in their place, can miss the bound.
Values may be sent and summed in bfloat16 or wider, within the bound.
A program may use at most 64 MiB of HBM per device.

v0:
```python
import functools
import math

import jax
import jax.numpy as jnp
from jax import lax
from jax.experimental import pallas as pl
from jax.experimental.pallas import tpu as pltpu
from jax.sharding import PartitionSpec as P

HEADS = 8
SUB = 8

epsilon = 1e-06
F32 = jnp.float32
BF16 = jnp.bfloat16


def dot_nn(a, b):
    return lax.dot_general(a, b, (((1,), (0,)), ((), ())), preferred_element_type=F32)


def dot_nt(a, b):
    return lax.dot_general(a, b, (((1,), (1,)), ((), ())), preferred_element_type=F32)


def flip(x):
    return x.astype(F32).T.astype(x.dtype)


def to_groups(x):
    members, cells, width = x.shape
    return jnp.concatenate(
        [x[:, i : i + SUB, :].reshape(members * SUB, width) for i in range(0, cells, SUB)], axis=0
    )


def from_groups(x, members, cells):
    width = x.shape[-1]
    size = members * SUB
    return jnp.concatenate(
        [x[g * size : (g + 1) * size].reshape(members, SUB, width) for g in range(cells // SUB)],
        axis=1,
    )


def attend_group(keys, vals, q_t, ga_t, k_t, v_t):
    tokens, width = keys.shape
    members = tokens // SUB
    head_dim = width // HEADS
    scale = 1.0 / math.sqrt(head_dim)
    head_of = lax.broadcasted_iota(jnp.int32, (tokens, width), 1) // head_dim
    row_cell = lax.broadcasted_iota(jnp.int32, (SUB, tokens), 0)
    col_cell = lax.broadcasted_iota(jnp.int32, (SUB, tokens), 1) % SUB
    same = (row_cell == col_cell)[None]
    outs = ([], [], [], [])
    for h in range(HEADS):
        own = head_of == h
        hs = slice(h * head_dim, (h + 1) * head_dim)
        k_own = jnp.where(own, keys.astype(F32), 0.0).astype(BF16)
        v_own = jnp.where(own, vals.astype(F32), 0.0).astype(BF16)
        scores = dot_nn(k_own, q_t).reshape(members, SUB, tokens) * scale
        grad_prob = dot_nn(v_own, ga_t).reshape(members, SUB, tokens)
        lifted = jnp.exp(scores - jnp.max(scores, axis=0, keepdims=True))
        prob = lifted * (1.0 / jnp.sum(lifted, axis=0, keepdims=True))
        inner = jnp.sum(prob * grad_prob, axis=0, keepdims=True)
        grad_score = prob * (grad_prob - inner) * scale
        prob_b = jnp.where(same, prob, 0.0).reshape(tokens, tokens).astype(BF16)
        gs_b = jnp.where(same, grad_score, 0.0).reshape(tokens, tokens).astype(BF16)
        outs[0].append(dot_nn(v_t[hs], prob_b))
        outs[1].append(dot_nn(k_t[hs], gs_b))
        outs[2].append(dot_nt(q_t[hs], gs_b))
        outs[3].append(dot_nt(ga_t[hs], prob_b))
    return tuple(jnp.concatenate(o, axis=0).astype(BF16) for o in outs)


def block_kernel(
    f_ref, gm_ref, gain_ref, wq_ref, wk_ref, wv_ref, wo_ref,
    corr_ref, mixed_ref, grads_ref, gain_out_ref,
):
    members, cells, width = f_ref.shape
    size = members * SUB
    flat = to_groups(f_ref[...].astype(F32))
    gm = to_groups(gm_ref[...].astype(F32)).astype(BF16)
    wq, wk, wv, wo = (w[...] for w in (wq_ref, wk_ref, wv_ref, wo_ref))
    inv = lax.rsqrt(jnp.mean(flat * flat, axis=-1, keepdims=True) + epsilon)
    normed = flat * inv
    inputs = (normed * gain_ref[...]).astype(BF16)
    in_t = flip(inputs)
    keys = dot_nn(inputs, wk).astype(BF16)
    vals = dot_nn(inputs, wv).astype(BF16)
    q_t = dot_nn(flip(wq), in_t).astype(BF16)
    k_t = dot_nn(flip(wk), in_t).astype(BF16)
    v_t = dot_nn(flip(wv), in_t).astype(BF16)
    ga_t = dot_nt(wo, gm).astype(BF16)
    parts = []
    for g in range(cells // SUB):
        rows = slice(g * size, (g + 1) * size)
        parts.append(
            attend_group(
                keys[rows], vals[rows], q_t[:, rows], ga_t[:, rows], k_t[:, rows], v_t[:, rows]
            )
        )
    att_t, gq_t, gk_t, gv_t = (jnp.concatenate(p, axis=1) for p in zip(*parts))
    mixed = dot_nn(flip(att_t), wo)
    mixed_ref[...] = from_groups(mixed, members, cells).astype(BF16)
    grad_in = (dot_nn(wq, gq_t) + dot_nn(wk, gk_t) + dot_nn(wv, gv_t)).T
    grads_ref[0:width] = dot_nt(in_t, gq_t)
    grads_ref[width : 2 * width] = dot_nt(in_t, gk_t)
    grads_ref[2 * width : 3 * width] = dot_nt(in_t, gv_t)
    grads_ref[3 * width : 4 * width] = dot_nn(att_t, gm)
    gain_out_ref[...] = jnp.sum(grad_in * normed, axis=0, keepdims=True)
    grad_normed = grad_in * gain_ref[...]
    corr = inv * (grad_normed - normed * jnp.mean(grad_normed * normed, axis=-1, keepdims=True))
    corr_ref[...] = from_groups(corr, members, cells).astype(BF16)


def block(f, gm, gain, wq, wk, wv, wo, interpret=False):
    width = f.shape[-1]
    return pl.pallas_call(
        block_kernel,
        out_shape=(
            jax.ShapeDtypeStruct(f.shape, BF16),
            jax.ShapeDtypeStruct(f.shape, BF16),
            jax.ShapeDtypeStruct((4 * width, width), F32),
            jax.ShapeDtypeStruct((1, width), F32),
        ),
        interpret=interpret,
        compiler_params=pltpu.CompilerParams(vmem_limit_bytes=48 * 2**20),
    )(f, gm, gain.reshape(1, -1), wq, wk, wv, wo)


MESH = pl.DeviceIdType.MESH
VMEM_SPEC = pl.BlockSpec(memory_space=pltpu.VMEM)


def enter(peers):
    barrier = pltpu.get_barrier_semaphore()
    for peer in peers:
        pl.semaphore_signal(barrier, inc=1, device_id=peer, device_id_type=MESH)
    pl.semaphore_wait(barrier, len(peers))


def push(src, dst, send_sem, recv_sem, peer):
    return pltpu.make_async_remote_copy(
        src_ref=src, dst_ref=dst, send_sem=send_sem, recv_sem=recv_sem,
        device_id=peer, device_id_type=MESH,
    )


def exchange_kernel(count, src, dst, send, recv):
    me = lax.axis_index("mem")
    row, col = lax.axis_index("row"), lax.axis_index("col")
    others = [lax.rem(me + k, count) for k in range(1, count)]
    enter([(o, row, col) for o in others])

    copies, arrivals = exchange_start(src, dst, send, recv, me, others, (row, col))
    exchange_finish(copies, arrivals)


def exchange_start(src, dst, send, recv, me, others, place):
    copies, arrivals = [], []
    for o in others:
        copy = push(src.at[o], dst.at[:, me], send.at[o], recv.at[me], (o, *place))
        copy.start()
        copies.append(copy)
        arrivals.append(push(src.at[o], dst.at[:, o], send.at[o], recv.at[o], (o, *place)))
    dst[:, me] = src[me]
    return copies, arrivals


def exchange_finish(copies, arrivals):
    for copy in copies:
        copy.wait_send()
    for arrival in arrivals:
        arrival.wait_recv()


def exchange(a, collective_id):
    count = lax.axis_size("mem")
    shape = a.shape
    out = (shape[1], shape[0]) + shape[2:]
    return pl.pallas_call(
        functools.partial(exchange_kernel, count),
        out_shape=jax.ShapeDtypeStruct(out, a.dtype),
        in_specs=[VMEM_SPEC],
        out_specs=VMEM_SPEC,
        scratch_shapes=[pltpu.SemaphoreType.DMA((count,))] * 2,
        compiler_params=pltpu.CompilerParams(collective_id=collective_id, has_side_effects=True),
    )(a)


def sum_kernel(
    count, planes, rows, cols, scale,
    g_ref, s_ref, x_ref, out_ref, sout_ref, x_out,
    a_src, a_dst, acc1, b_src, b_dst, acc2, c_src, c_dst, gz, gp, ga, s_a, s_b, s_c,
    send_a, recv_a, send_b, recv_b, send_c, recv_c,
    send_z, recv_z, send_p, recv_p, send_g, recv_g,
    ssend_b, srecv_b, ssend_c, srecv_c, ssend_a, srecv_a, xsend, xrecv,
):
    mem, row, col = (lax.axis_index(a) for a in ("mem", "row", "col"))
    core = lax.rem(mem, 2)
    other = 1 - core
    me_p = lax.div(mem, 2) * cols + col
    partner = (mem + 1 - 2 * core, row, col)

    def plane_peer(p):
        return (lax.div(p, cols) * 2 + core, row, lax.rem(p, cols))

    plane_others = [lax.rem(me_p + k, planes) for k in range(1, planes)]
    row_others = [lax.rem(row + k, rows) for k in range(1, rows)]
    mem_others = [lax.rem(mem + k, count) for k in range(1, count)]
    enter(
        [(o, row, col) for o in mem_others]
        + [partner]
        + [plane_peer(p) for p in plane_others]
        + [(mem, r, col) for r in row_others]
    )

    a_src[...] = g_ref[other].astype(BF16)
    first = push(a_src, a_dst, send_a, recv_a, partner)
    first.start()
    s_a[core] = s_ref[...]
    small = push(s_a.at[core], s_a.at[core], ssend_a, srecv_a, partner)
    small.start()
    moving = exchange_start(x_ref, x_out, xsend, xrecv, mem, mem_others, (row, col))
    first.wait()
    acc1[...] = g_ref[core] + a_dst[...].astype(F32)
    b_src[...] = acc1[...].astype(BF16)

    sent = []
    for p in plane_others:
        copy = push(b_src.at[p], b_dst.at[me_p], send_b.at[p], recv_b.at[me_p], plane_peer(p))
        copy.start()
        sent.append(copy)
    small.wait_send()
    push(s_a.at[other], s_a.at[other], ssend_a, srecv_a, partner).wait_recv()
    s_b[me_p] = s_a[0] + s_a[1]
    for p in plane_others:
        copy = push(s_b.at[me_p], s_b.at[me_p], ssend_b.at[p], srecv_b.at[me_p], plane_peer(p))
        copy.start()
        sent.append(copy)
    acc2[...] = acc1[me_p]
    for p in plane_others:
        push(b_src.at[p], b_dst.at[p], send_b.at[p], recv_b.at[p], plane_peer(p)).wait_recv()
        acc2[...] += b_dst[p].astype(F32)
    c_src[...] = acc2[...].astype(BF16)

    for r in row_others:
        copy = push(c_src.at[r], c_dst.at[row], send_c.at[r], recv_c.at[row], (mem, r, col))
        copy.start()
        sent.append(copy)
    for p in plane_others:
        push(s_b.at[p], s_b.at[p], ssend_b.at[p], srecv_b.at[p], plane_peer(p)).wait_recv()
    total = s_b[0]
    for p in range(1, planes):
        total = total + s_b[p]
    s_c[row] = total
    for r in row_others:
        copy = push(s_c.at[row], s_c.at[row], ssend_c.at[r], srecv_c.at[row], (mem, r, col))
        copy.start()
        sent.append(copy)
    whole = acc2[row]
    for r in row_others:
        push(c_src.at[r], c_dst.at[r], send_c.at[r], recv_c.at[r], (mem, r, col)).wait_recv()
        whole = whole + c_dst[r].astype(F32)
    gz[row] = (whole * scale).astype(BF16)

    for r in row_others:
        copy = push(gz.at[row], gz.at[row], send_z.at[r], recv_z.at[row], (mem, r, col))
        copy.start()
        sent.append(copy)
    for r in row_others:
        push(s_c.at[r], s_c.at[r], ssend_c.at[r], srecv_c.at[r], (mem, r, col)).wait_recv()
    total = s_c[0]
    for r in range(1, rows):
        total = total + s_c[r]
    sout_ref[...] = total * scale
    for r in row_others:
        push(gz.at[r], gz.at[r], send_z.at[r], recv_z.at[r], (mem, r, col)).wait_recv()
    for p in plane_others:
        copy = push(gz, gp.at[me_p], send_p.at[p], recv_p.at[me_p], plane_peer(p))
        copy.start()
        sent.append(copy)
    own = push(gz, ga.at[me_p], send_g.at[me_p], recv_g.at[me_p], partner)
    own.start()
    sent.append(own)
    out_ref[core, me_p] = gz[...].astype(F32)
    for p in plane_others:
        push(gz, gp.at[p], send_p.at[p], recv_p.at[p], plane_peer(p)).wait_recv()
        copy = push(gp.at[p], ga.at[p], send_g.at[p], recv_g.at[p], partner)
        copy.start()
        sent.append(copy)
        out_ref[core, p] = gp[p].astype(F32)
    for p in [me_p] + plane_others:
        push(gz, ga.at[p], send_g.at[p], recv_g.at[p], partner).wait_recv()
        out_ref[other, p] = ga[p].astype(F32)
    for copy in sent:
        copy.wait_send()
    exchange_finish(*moving)


def sum_all(grads, small, x, scale, collective_id):
    count = lax.axis_size("mem")
    x_shape = (x.shape[1], x.shape[0]) + x.shape[2:]
    rows, cols = lax.axis_size("row"), lax.axis_size("col")
    planes = lax.axis_size("mem") // 2 * cols
    height, width = grads.shape
    unit = (height // (2 * planes * rows), width)
    part, half = (rows,) + unit, (planes, rows) + unit
    full = (2,) + half
    sems = pltpu.SemaphoreType.DMA
    out, sout, x = pl.pallas_call(
        functools.partial(sum_kernel, count, planes, rows, cols, scale),
        out_shape=(
            jax.ShapeDtypeStruct(full, F32),
            jax.ShapeDtypeStruct(small.shape, F32),
            jax.ShapeDtypeStruct(x_shape, x.dtype),
        ),
        in_specs=[VMEM_SPEC] * 3,
        out_specs=(VMEM_SPEC,) * 3,
        scratch_shapes=[
            pltpu.VMEM(half, BF16), pltpu.VMEM(half, BF16), pltpu.VMEM(half, F32),
            pltpu.VMEM(half, BF16), pltpu.VMEM(half, BF16), pltpu.VMEM(part, F32),
            pltpu.VMEM(part, BF16), pltpu.VMEM(part, BF16), pltpu.VMEM(part, BF16),
            pltpu.VMEM(half, BF16), pltpu.VMEM(half, BF16),
            pltpu.VMEM((2,) + small.shape, F32),
            pltpu.VMEM((planes,) + small.shape, F32),
            pltpu.VMEM((rows,) + small.shape, F32),
            sems(()), sems(()), sems((planes,)), sems((planes,)), sems((rows,)), sems((rows,)),
            sems((rows,)), sems((rows,)), sems((planes,)), sems((planes,)),
            sems((planes,)), sems((planes,)),
            sems((planes,)), sems((planes,)), sems((rows,)), sems((rows,)), sems(()), sems(()),
            sems((count,)), sems((count,)),
        ],
        compiler_params=pltpu.CompilerParams(
            collective_id=collective_id, has_side_effects=True, vmem_limit_bytes=48 * 2**20
        ),
    )(grads.reshape(full), small, x)
    return out.reshape(height, width), sout, x

NEAR = [(dr, dc) for dr in (-1, 0, 1) for dc in (-1, 0, 1) if (dr, dc) != (0, 0)]
EDGE = 8


def entry_kernel(
    count, grid,
    f_ref, cot_ref, edges_ref, taps_ref, f_out, gm_out, pad_out,
    row_halo, col_halo, pad, gm_src, send, recv, near_send, near_recv,
):
    members, rows, cols, width = cot_ref.shape
    me = lax.axis_index("mem")
    at = (lax.axis_index("row"), lax.axis_index("col"))
    others = [lax.rem(me + k, count) for k in range(1, count)]

    def exists(step):
        tests = [
            (at[i] > 0) if step[i] < 0 else (at[i] < grid[i] - 1) for i in range(2) if step[i]
        ]
        return functools.reduce(jnp.logical_and, tests)

    def neighbour(step):
        return (me, at[0] + step[0], at[1] + step[1])

    def outgoing(step):
        dr, dc = step
        if dc == 0:
            return cot_ref.at[:, 0 if dr < 0 else rows - 1]
        side = edges_ref.at[0 if dc < 0 else 1]
        return side if dr == 0 else side.at[0 if dr < 0 else rows - 1]

    def landing(step):
        dr, dc = step
        if dc == 0:
            return row_halo.at[0 if dr < 0 else 1]
        side = col_halo.at[0 if dc < 0 else 1]
        return side.at[pl.ds(1, rows)] if dr == 0 else side.at[0 if dr < 0 else rows + 1]

    def halo_copy(i):
        step = NEAR[i]
        back = len(NEAR) - 1 - i
        return push(
            outgoing(step), landing(NEAR[back]), near_send.at[i], near_recv.at[back],
            neighbour(step),
        )

    barrier = pltpu.get_barrier_semaphore()
    for o in others:
        pl.semaphore_signal(barrier, inc=1, device_id=(o, *at), device_id_type=MESH)
    for step in NEAR:
        @pl.when(exists(step))
        def _():
            pl.semaphore_signal(barrier, inc=1, device_id=neighbour(step), device_id_type=MESH)
    present = sum(exists(step).astype(jnp.int32) for step in NEAR)
    pl.semaphore_wait(barrier, present + len(others))

    for i in range(len(NEAR)):
        @pl.when(exists(NEAR[i]))
        def _():
            halo_copy(i).start()

        @pl.when(jnp.logical_not(exists(NEAR[i])))
        def _():
            there = landing(NEAR[i])
            there[...] = jnp.zeros(there.shape, BF16)
    srcs, dsts = (f_ref, gm_src), (f_out, gm_out)

    def spread(t):
        copies = []
        for o in others:
            copy = push(
                srcs[t].at[:, o], dsts[t].at[me], send.at[t, o], recv.at[t, me], (o, *at)
            )
            copy.start()
            copies.append(copy)
        dsts[t][me] = srcs[t][:, me]
        return copies

    copies = spread(0)
    pad[:, 1 : rows + 1, EDGE : EDGE + cols, :] = cot_ref[...].astype(F32)
    for i in range(len(NEAR)):
        @pl.when(exists(NEAR[i]))
        def _():
            there = landing(NEAR[i])
            push(
                there, there, near_send.at[i], near_recv.at[i], neighbour(NEAR[i])
            ).wait_recv()
    pad[:, 0, EDGE : EDGE + cols, :] = row_halo[0].astype(F32)
    pad[:, rows + 1, EDGE : EDGE + cols, :] = row_halo[1].astype(F32)
    for side, place in ((0, EDGE - 1), (1, EDGE + cols)):
        for r in range(rows + 2):
            column = col_halo[side, r].astype(F32)
            for m in range(members):
                pad[m, r, place : place + 1, :] = column[m : m + 1]
    for m in range(members):
        summed = jnp.zeros((rows, cols, width), F32)
        for i in range(3):
            for j in range(3):
                first = EDGE + 1 - j
                summed = summed + taps_ref[3 * i + j : 3 * i + j + 1, :] * pad[
                    m, 2 - i : 2 - i + rows, first : first + cols, :
                ]
        gm_src[m] = summed.reshape(gm_src.shape[1:]).astype(BF16)
    copies += spread(1)
    pad_out[...] = pad[:, :, EDGE - 1 : EDGE + 1 + cols, :].astype(BF16)
    for i in range(len(NEAR)):
        @pl.when(exists(NEAR[i]))
        def _():
            halo_copy(i).wait_send()
    for copy in copies:
        copy.wait_send()
    for t in range(2):
        for o in others:
            push(
                srcs[t].at[:, o], dsts[t].at[o], send.at[t, o], recv.at[t, o], (o, *at)
            ).wait_recv()


def entry(fields, cotangent, taps, collective_id):
    count = lax.axis_size("mem")
    members, rows, cols, width = fields.shape
    cells = rows * cols // count
    split = (members, count, cells, width)
    got = (count, members, cells, width)
    edges = jnp.swapaxes(jnp.stack([cotangent[:, :, 0], cotangent[:, :, -1]]), 1, 2)
    sems = pltpu.SemaphoreType.DMA
    return pl.pallas_call(
        functools.partial(entry_kernel, count, (lax.axis_size("row"), lax.axis_size("col"))),
        out_shape=(
            jax.ShapeDtypeStruct(got, BF16),
            jax.ShapeDtypeStruct(got, BF16),
            jax.ShapeDtypeStruct((members, rows + 2, cols + 2, width), BF16),
        ),
        in_specs=[VMEM_SPEC] * 4,
        out_specs=(VMEM_SPEC,) * 3,
        scratch_shapes=[
            pltpu.VMEM((2, members, cols, width), BF16),
            pltpu.VMEM((2, rows + 2, members, width), BF16),
            pltpu.VMEM((members, rows + 2, cols + 2 * EDGE, width), F32),
            pltpu.VMEM(split, BF16),
            sems((2, count)), sems((2, count)), sems((len(NEAR),)), sems((len(NEAR),)),
        ],
        compiler_params=pltpu.CompilerParams(
            collective_id=collective_id, has_side_effects=True, vmem_limit_bytes=48 * 2**20
        ),
    )(fields.reshape(split), cotangent, edges, taps)


def local(fields, norm_gain, w_query, w_key, w_value, w_out, mix_kernel, cotangent):
    members, tile_rows, tile_cols, width = fields.shape
    cells = tile_rows * tile_cols
    count = lax.axis_size("mem")
    f_got, gm_got, padded_cot = entry(fields, cotangent, mix_kernel.reshape(9, width), 1)
    shifts = [
        padded_cot[:, 2 - i : 2 - i + tile_rows, 2 - j : 2 - j + tile_cols, :].astype(F32)
        for i in range(3)
        for j in range(3)
    ]
    joined = (members * count, cells // count, width)
    corr, mixed, grads, gain = block(
        f_got.reshape(joined), gm_got.reshape(joined), norm_gain, w_query, w_key, w_value, w_out
    )
    sender = (count, members, cells // count, width)
    mixed = exchange(mixed.reshape(sender), 2)
    mixed = mixed.reshape(fields.shape).astype(F32)
    terms = [jnp.sum(s * mixed, axis=(0, 1, 2))[None] for s in shifts]
    small = jnp.concatenate([gain, *terms, jnp.zeros((6, width), F32)])
    tokens = math.prod(fields.shape[:3]) * math.prod(
        lax.axis_size(a) for a in ("mem", "row", "col")
    )
    total, small, corr = sum_all(grads, small, corr.reshape(sender), 1.0 / math.sqrt(tokens), 3)
    grad_fields = (cotangent.astype(F32) + corr.reshape(fields.shape).astype(F32)).astype(BF16)
    w = [total[i * width : (i + 1) * width] for i in range(4)]
    return (grad_fields, small[0], *w, small[1:10].reshape(3, 3, width))


def solution(mesh):
    tile = P("mem", "row", "col", None)
    in_specs = (tile, P(), P(), P(), P(), P(), P(), tile)
    out_specs = (tile, P(), P(), P(), P(), P(), P())
    return jax.shard_map(local, mesh=mesh, in_specs=in_specs, out_specs=out_specs, check_vma=False)
```

profile of v0, /device:TPU:0, one launch (start us, length us, event | category | flops | bytes accessed | tf_op | source)
XLA Modules:
  0.0 64.2 jit_solution(13598561301301055667)
XLA Ops:
  0.6 0.7 %reshape.41.taps_ref = f32[9,256]{1,0:T(8,128)S(1)} reshape(f32[3,3,256]{2,1,0:T(4,128)} %param.14) | data formatting | bytes 18432 | tf_op jit(solution)/shard_map/reshape | solution.py:493
  1.3 0.9 %fusion.10 = (bf16[4,4,1,256]{3,2,1,0:T(2,128)(2,1)S(1)}, bf16[4,4,1,256]{3,2,1,0:T(2,128)(2,1)S(1)}) fusion(bf16[4,4,32,256]{3,2,1,0:T(8,128)(2,1)} %cot_ref.1), kind=kLoop, calls=%fused_computation.23 | loop fusion | bytes 32768 | tf_op jit(solution)/shard_map/slice | solution.py:465
  2.3 0.0 copy-start
  2.3 0.9 %copy-done = bf16[4,4,32,256]{3,2,1,0:T(8,128)(2,1)S(1)} copy-done((bf16[4,4,32,256]{3,2,1,0:T(8,128)(2,1)S(1)}, bf16[4,4,32,256]{3,2,1,0:T(8,128)(2,1)}, u32[]{:S(2)}) %copy-start) | copy-done | bytes 262168
  3.3 0.9 %copy-done.2 = bf16[4,4,32,256]{3,2,1,0:T(8,128)(2,1)S(1)} copy-done((bf16[4,4,32,256]{3,2,1,0:T(8,128)(2,1)S(1)}, bf16[4,4,32,256]{3,2,1,0:T(8,128)(2,1)}, u32[]{:S(2)}) %copy-start.2) | copy-done | bytes 262168
  4.2 12.7 %shard_map.135 = (bf16[4,4,32,256]{3,2,1,0:T(8,128)(2,1)S(1)}, bf16[4,4,32,256]{3,2,1,0:T(8,128)(2,1)S(1)}, bf16[4,6,34,256]{3,2,1,0:T(8,128)(2,1)S(1)}) custom-call(bf16[4,4,32,256]{3,2,1,0:T(8,128)(2,1)S(1)} %copy-done.2, bf16[4,4,32,256]{3,2,1,0:T(8,128)(2,1)S(1)} %copy-done, bf16[2,4,4,256]{3,2,1,0:T(4,128)(2,1)S(1)} %maximum_bitcast_fusion.edges_ref, ...), custom_call_target="tpu_custom_call" | custom-call | tf_op jit(solution)/shard_map/pallas_call | solution.py:467
  16.9 0.0 copy-start.8
  16.9 0.0 copy-done.4
  16.9 0.0 copy-done.5
  17.0 0.0 copy-done.6
  17.0 0.0 copy-done.7
  17.0 0.6 copy-done.8
  17.6 9.7 %shard_map.136 = (bf16[16,32,256]{2,1,0:T(8,128)(2,1)S(1)}, bf16[16,32,256]{2,1,0:T(8,128)(2,1)S(1)}, f32[1024,256]{1,0:T(8,128)S(1)}, f32[1,256]{1,0:T(1,128)S(1)}) custom-call(bf16[16,32,256]{2,1,0:T(8,128)(2,1)S(1)} %bitcast.25, bf16[16,32,256]{2,1,0:T(8,128)(2,1)S(1)} %bitcast.26, f32[1,256]{1,0:T(1,128)S(1)} %bitcast.29, ...), custom_call_target="tpu_custom_call" | custom-call | tf_op jit(solution)/shard_map/pallas_call | solution.py:120
  27.3 0.0 copy-start.3
  27.3 0.7 %copy-done.3 = bf16[16,32,256]{2,1,0:T(8,128)(2,1)} copy-done((bf16[16,32,256]{2,1,0:T(8,128)(2,1)}, bf16[16,32,256]{2,1,0:T(8,128)(2,1)S(1)}, u32[]{:S(2)}) %copy-start.3) | copy-done | bytes 262168
  28.0 6.8 %shard_map.137 = bf16[4,4,32,256]{3,2,1,0:T(8,128)(2,1)} custom-call(bf16[4,4,32,256]{3,2,1,0:T(8,128)(2,1)} %bitcast.27), custom_call_target="tpu_custom_call" | custom-call | tf_op jit(solution)/shard_map/pallas_call | solution.py:183
  34.8 1.5 %fusion.8 = (f32[256]{0:T(256)S(1)}, f32[256]{0:T(256)S(1)}, f32[256]{0:T(256)S(1)}, f32[256]{0:T(256)S(1)}, f32[256]{0:T(256)S(1)}, /*index=5*/f32[256]{0:T(256...) fusion(bf16[4,4,32,256]{3,2,1,0:T(8,128)(2,1)} %shard_map.137, bf16[4,6,34,256]{3,2,1,0:T(8,128)(2,1)S(1)} %get-tuple-element.21), kind=kLoop, calls=%fused_computation.17 | loop fusion | flops 3667712 | bytes 2630656 | tf_op jit(solution)/shard_map/reduce_sum | solution.py:506
  36.3 0.1 concatenate.3.s_ref
  36.4 24.8 %shard_map.138 = (f32[2,4,4,32,256]{4,3,2,1,0:T(8,128)S(1)}, f32[16,256]{1,0:T(8,128)S(1)}, bf16[4,4,32,256]{3,2,1,0:T(8,128)(2,1)S(1)}) custom-call(f32[2,4,4,32,256]{4,3,2,1,0:T(8,128)S(1)} %bitcast.23, f32[16,256]{1,0:T(8,128)S(1)} %concatenate.3.s_ref, bf16[4,4,32,256]{3,2,1,0:T(8,128)(2,1)S(1)} %bitcast.28), custom_call_target="tpu_custom_call" | custom-call | tf_op jit(solution)/shard_map/pallas_call | solution.py:313
  61.2 0.0 copy-done.1
  61.2 0.8 %add_convert_fusion = bf16[4,4,32,256]{3,2,1,0:T(8,128)(2,1)} fusion(bf16[4,4,32,256]{3,2,1,0:T(8,128)(2,1)S(1)} %get-tuple-element.24, bf16[4,4,32,256]{3,2,1,0:T(8,128)(2,1)S(1)} %copy-done.1), kind=kLoop, calls=%fused_computation.18 | loop fusion | flops 524288 | bytes 786432 | tf_op jit(solution)/shard_map/convert_element_type | solution.py:512
  62.0 1.0 %fusion.9 = (f32[256,256]{1,0:T(8,128)}, f32[256,256]{1,0:T(8,128)}, f32[256,256]{1,0:T(8,128)}, f32[256,256]{1,0:T(8,128)}) fusion(f32[1024,256]{1,0:T(8,128)S(1)} %bitcast.24), kind=kLoop, calls=%fused_computation.22 | loop fusion | bytes 2097152 | tf_op jit(solution)/shard_map/slice | solution.py:513
  63.0 0.6 slice.62
  63.6 0.6 reshape.49
  (10 shorter events, 0.0 us)
Async XLA Ops:
  2.3 1.0 %copy-start = (bf16[4,4,32,256]{3,2,1,0:T(8,128)(2,1)S(1)}, bf16[4,4,32,256]{3,2,1,0:T(8,128)(2,1)}, u32[]{:S(2)}) copy-start(bf16[4,4,32,256]{3,2,1,0:T(8,128)(2,1)} %cot_ref.1) | copy-start | bytes 786436
  3.2 0.9 %copy-start.2 = (bf16[4,4,32,256]{3,2,1,0:T(8,128)(2,1)S(1)}, bf16[4,4,32,256]{3,2,1,0:T(8,128)(2,1)}, u32[]{:S(2)}) copy-start(bf16[4,4,32,256]{3,2,1,0:T(8,128)(2,1)} %f_ref.1) | copy-start | bytes 786436
  4.2 12.7 %copy-start.4 = (bf16[256,256]{1,0:T(8,128)(2,1)S(1)}, bf16[256,256]{1,0:T(8,128)(2,1)}, u32[]{:S(2)}) copy-start(bf16[256,256]{1,0:T(8,128)(2,1)} %wq_ref.1) | copy-start | bytes 393220
  4.2 12.7 %copy-start.5 = (bf16[256,256]{1,0:T(8,128)(2,1)S(1)}, bf16[256,256]{1,0:T(8,128)(2,1)}, u32[]{:S(2)}) copy-start(bf16[256,256]{1,0:T(8,128)(2,1)} %wk_ref.1) | copy-start | bytes 393220
  4.2 12.8 %copy-start.6 = (bf16[256,256]{1,0:T(8,128)(2,1)S(1)}, bf16[256,256]{1,0:T(8,128)(2,1)}, u32[]{:S(2)}) copy-start(bf16[256,256]{1,0:T(8,128)(2,1)} %wv_ref.1) | copy-start | bytes 393220
  4.2 12.8 %copy-start.7 = (bf16[256,256]{1,0:T(8,128)(2,1)S(1)}, bf16[256,256]{1,0:T(8,128)(2,1)}, u32[]{:S(2)}) copy-start(bf16[256,256]{1,0:T(8,128)(2,1)} %wo_ref.1) | copy-start | bytes 393220
  16.9 0.7 %copy-start.8 = (f32[256]{0:T(256)S(1)}, f32[256]{0:T(256)}, u32[]{:S(2)}) copy-start(f32[256]{0:T(256)} %param.9) | copy-start | bytes 3076
  27.3 0.7 %copy-start.3 = (bf16[16,32,256]{2,1,0:T(8,128)(2,1)}, bf16[16,32,256]{2,1,0:T(8,128)(2,1)S(1)}, u32[]{:S(2)}) copy-start(bf16[16,32,256]{2,1,0:T(8,128)(2,1)S(1)} %get-tuple-element.22) | copy-start | bytes 786436
  36.4 24.8 %copy-start.1 = (bf16[4,4,32,256]{3,2,1,0:T(8,128)(2,1)S(1)}, bf16[4,4,32,256]{3,2,1,0:T(8,128)(2,1)}, u32[]{:S(2)}) copy-start(bf16[4,4,32,256]{3,2,1,0:T(8,128)(2,1)} %cot_ref.1) | copy-start | bytes 786436
where the time goes:
time: 64.5 us; the launch traced here: 64.2 us
  Pallas kernels  54 us (84%)
  local copies, waits for them, and re-layouts  7.08 us (11%)
  other arithmetic  2.3 us (4%)
  between operations  0.76 us (1%)
    pallas_call x1, Pallas kernels, sum_all(): pl.pallas_call(functools.partial(sum_kernel, count, planes, rows, cols, s...  24.8 us
    pallas_call x1, Pallas kernels, entry(): pl.pallas_call(functools.partial(entry_kernel, count, (lax.axis_size('row...  12.7 us
    pallas_call x1, Pallas kernels, block(): pl.pallas_call(block_kernel, out_shape=(jax.ShapeDtypeStruct(f.shape, BF1...  9.69 us
    pallas_call x1, Pallas kernels, exchange(): pl.pallas_call(functools.partial(exchange_kernel, count), out_shape=jax.S...  6.8 us
    unnamed x18, local copies, waits for them, and re-layouts  3.24 us
    reduce_sum x1, other arithmetic, local(): terms = [jnp.sum(s * mixed, axis=(0, 1, 2))[None] for s in shifts]  1.5 us

commit v1 on v0

v1 whole, which is shorter than its diff:
```python
import functools
import math

import jax
import jax.numpy as jnp
from jax import lax
from jax.experimental import pallas as pl
from jax.experimental.pallas import tpu as pltpu
from jax.sharding import PartitionSpec as P

HEADS = 8
SUB = 8
BLOCK = 16
EDGE = 8

epsilon = 1e-06
F32 = jnp.float32
BF16 = jnp.bfloat16
MESH = pl.DeviceIdType.MESH
VMEM_SPEC = pl.BlockSpec(memory_space=pltpu.VMEM)
HBM_SPEC = pl.BlockSpec(memory_space=pltpu.HBM)
NEAR = [(dr, dc) for dr in (-1, 0, 1) for dc in (-1, 0, 1) if (dr, dc) != (0, 0)]


def dot_nn(a, b):
    return lax.dot_general(a, b, (((1,), (0,)), ((), ())), preferred_element_type=F32)


def dot_nt(a, b):
    return lax.dot_general(a, b, (((1,), (1,)), ((), ())), preferred_element_type=F32)


def one_hot(size, target):
    row = lax.broadcasted_iota(jnp.int32, (size, size), 0)
    col = lax.broadcasted_iota(jnp.int32, (size, size), 1)
    return jnp.where(target(row) == col, 1.0, 0.0).astype(BF16)


def cell_first(members):
    size = members * BLOCK
    there = one_hot(size, lambda i: lax.rem(i, members) * BLOCK + lax.div(i, members))
    back = one_hot(size, lambda i: lax.rem(i, BLOCK) * members + lax.div(i, BLOCK))
    return there, back


def cell_masks(members):
    tokens = SUB * members
    lane = lax.div(lax.broadcasted_iota(jnp.int32, (members, tokens), 1), members)
    own = [lane == c for c in range(SUB)]
    return own, [jnp.where(o, 1.0, 0.0).astype(BF16) for o in own]


def own_cells(left, right_t, own):
    tokens, width = left.shape
    members = tokens // SUB
    dim = width // HEADS
    zeros = jnp.zeros((dim, tokens), right_t.dtype)
    heads = []
    for h in range(0, HEADS, 2):
        pair = [
            jnp.concatenate(
                [right_t[k * dim : (k + 1) * dim] if k == p else zeros for k in range(HEADS)], axis=0
            )
            for p in (h, h + 1)
        ]
        both = dot_nn(left, jnp.concatenate(pair, axis=1))
        for i in range(2):
            full = both[:, i * tokens : (i + 1) * tokens]
            picked = full[:members]
            for c in range(1, SUB):
                picked = jnp.where(own[c], full[c * members : (c + 1) * members], picked)
            heads.append(picked)
    return jnp.stack(heads)


def spread(packed, mask):
    return jnp.concatenate([packed * m for m in mask], axis=0)


def softmax_group(keys, q_t, own):
    dim = keys.shape[1] // HEADS
    scores = own_cells(keys, q_t, own) * (1.0 / math.sqrt(dim))
    lifted = jnp.exp(scores - jnp.max(scores, axis=1, keepdims=True))
    return lifted * (1.0 / jnp.sum(lifted, axis=1, keepdims=True))


def attend_group(prob, v_t, mask):
    dim = v_t.shape[0] // HEADS
    return jnp.concatenate(
        [
            dot_nn(v_t[h * dim : (h + 1) * dim], spread(prob[h].astype(BF16), mask))
            for h in range(HEADS)
        ],
        axis=0,
    ).astype(BF16)


def back_group(prob, vals, q_t, ga_t, k_t, own, mask):
    dim = vals.shape[1] // HEADS
    grad_prob = own_cells(vals, ga_t, own)
    inner = jnp.sum(prob * grad_prob, axis=1, keepdims=True)
    grad_score = prob * (grad_prob - inner) * (1.0 / math.sqrt(dim))
    outs = ([], [], [])
    for h in range(HEADS):
        hs = slice(h * dim, (h + 1) * dim)
        gs = spread(grad_score[h].astype(BF16), mask)
        pb = spread(prob[h].astype(BF16), mask)
        outs[0].append(dot_nn(k_t[hs], gs))
        outs[1].append(dot_nt(q_t[hs], gs))
        outs[2].append(dot_nt(ga_t[hs], pb))
    return tuple(jnp.concatenate(o, axis=0).astype(BF16) for o in outs)


def groups_of(tokens, members):
    size = SUB * members
    return [slice(i, i + size) for i in range(0, tokens, size)]


def forward_block(x, gain, wq_t, wk_t, wv_t, wk, wv, wo, there, back, eye, own, mask):
    tokens = x.shape[0]
    members = tokens // BLOCK
    inv = lax.rsqrt(jnp.mean(x * x, axis=-1, keepdims=True) + epsilon)
    normed = x * inv
    inputs = dot_nn(there, (normed * gain).astype(BF16)).astype(BF16)
    keys = dot_nn(inputs, wk).astype(BF16)
    vals = dot_nn(inputs, wv).astype(BF16)
    q_t = dot_nt(wq_t, inputs).astype(BF16)
    k_t = dot_nt(wk_t, inputs).astype(BF16)
    v_t = dot_nt(wv_t, inputs).astype(BF16)
    in_t = dot_nt(eye, inputs).astype(BF16)
    probs, parts = [], []
    for s in groups_of(tokens, members):
        prob = softmax_group(keys[s], q_t[:, s], own)
        probs.append(prob)
        parts.append(attend_group(prob, v_t[:, s], mask))
    att_t = jnp.concatenate(parts, axis=1)
    mixed = dot_nn(dot_nt(back, att_t).astype(BF16), wo).astype(BF16)
    return mixed, (inv, normed, vals, q_t, k_t, in_t, att_t, probs)


def backward_block(gm, saved, wo, there, own, mask):
    inv, normed, vals, q_t, k_t, in_t, att_t, probs = saved
    tokens = gm.shape[0]
    gm = dot_nn(there, gm).astype(BF16)
    ga_t = dot_nt(wo, gm).astype(BF16)
    parts = [
        back_group(prob, vals[s], q_t[:, s], ga_t[:, s], k_t[:, s], own, mask)
        for s, prob in zip(groups_of(tokens, tokens // BLOCK), probs)
    ]
    return (gm,) + tuple(jnp.concatenate(p, axis=1) for p in zip(*parts))


def input_block(gq_t, gk_t, gv_t, saved, gain, wq, wk, wv, back):
    inv, normed = saved[:2]
    rows = [dot_nt(back, g).astype(BF16) for g in (gq_t, gk_t, gv_t)]
    grad_in = dot_nt(rows[0], wq) + dot_nt(rows[1], wk) + dot_nt(rows[2], wv)
    grad_normed = grad_in * gain
    corr = inv * (grad_normed - normed * jnp.mean(grad_normed * normed, axis=-1, keepdims=True))
    return corr.astype(BF16), jnp.sum(grad_in * normed, axis=0, keepdims=True)


def push(src, dst, send_sem, recv_sem, peer):
    return pltpu.make_async_remote_copy(
        src_ref=src, dst_ref=dst, send_sem=send_sem, recv_sem=recv_sem,
        device_id=peer, device_id_type=MESH,
    )


def main_kernel(
    sizes, scale,
    f_hbm, cot_hbm, gain_hbm, wq_hbm, wk_hbm, wv_hbm, wo_hbm, taps_hbm,
    gf_ref, out_ref, small_ref,
    cot, gain_v, wq_v, wk_v, wv_v, wo_v, taps, f_got, gm_src, gm_got, mx_src, mx_got,
    co_src, co_got, row_halo, edges, col_halo, pad,
    g, a_src, a_dst, acc1, b_src, b_dst, c_src, c_dst, ga, s_a, s_b, s_c,
    load, near_send, near_recv, f_send, f_recv, gm_send, gm_recv, mx_send, mx_recv,
    co_send, co_recv, a_send, a_recv, b_send, b_recv, c_send, c_recv, z_send, z_recv,
    p_send, p_recv, g_send, g_recv,
    sa_send, sa_recv, sb_send, sb_recv, sc_send, sc_recv,
):
    count, grid_rows, grid_cols = sizes
    members, rows, cols, width = cot.shape
    cells = f_got.shape[2]
    planes = count // 2 * grid_cols
    unit = g.shape[3]
    mem, row, col = (lax.axis_index(a) for a in ("mem", "row", "col"))
    at = (row, col)
    core, chip = lax.rem(mem, 2), lax.div(mem, 2)
    other = 1 - core
    partner = (mem + 1 - 2 * core, row, col)
    me_p = chip * grid_cols + col

    def plane_peer(p):
        return (lax.div(p, grid_cols) * 2 + core, row, lax.rem(p, grid_cols))

    mem_others = [lax.rem(mem + k, count) for k in range(1, count)]
    plane_others = [lax.rem(me_p + k, planes) for k in range(1, planes)]
    step_z = 1 - 2 * lax.div(row * 2, grid_rows)
    row_others = [
        lax.rem(row + step_z * k + grid_rows, grid_rows) for k in range(1, grid_rows)
    ]

    local = [
        pltpu.make_async_copy(cot_hbm, cot, load.at[0]),
        pltpu.make_async_copy(taps_hbm, taps, load.at[1]),
        pltpu.make_async_copy(wq_hbm, wq_v, load.at[2]),
        pltpu.make_async_copy(wk_hbm, wk_v, load.at[3]),
        pltpu.make_async_copy(wv_hbm, wv_v, load.at[4]),
        pltpu.make_async_copy(wo_hbm, wo_v, load.at[5]),
        pltpu.make_async_copy(gain_hbm, gain_v, load.at[6]),
        pltpu.make_async_copy(f_hbm.at[:, mem], f_got.at[mem], load.at[7]),
    ]
    for copy in local:
        copy.start()

    def exists(step):
        tests = [
            (at[i] > 0) if step[i] < 0 else (at[i] < (grid_rows, grid_cols)[i] - 1)
            for i in range(2)
            if step[i]
        ]
        return functools.reduce(jnp.logical_and, tests)

    def neighbour(step):
        return (mem, row + step[0], col + step[1])

    barrier = pltpu.get_barrier_semaphore()

    def greet(peer):
        pl.semaphore_signal(barrier, inc=1, device_id=peer, device_id_type=MESH)

    greeted = 0
    for r in row_others:
        greet((mem, r, col))
        greeted += 1
    for o in mem_others:
        greet((o, row, col))
        greeted += 1
    for k in range(count // 2):
        for c in range(1, grid_cols):
            there_chip = lax.rem(chip + k, count // 2)
            greet((there_chip * 2 + core, row, lax.rem(col + c, grid_cols)))
            greeted += 1
    diagonal = [step for step in NEAR if step[0] and step[1]]
    for step in diagonal:
        @pl.when(exists(step))
        def _():
            greet(neighbour(step))
    present = sum(exists(step).astype(jnp.int32) for step in diagonal)

    def outgoing(step):
        dr, dc = step
        if dc == 0:
            return cot.at[:, 0 if dr < 0 else rows - 1]
        side = edges.at[0 if dc < 0 else 1]
        return side if dr == 0 else side.at[0 if dr < 0 else rows - 1]

    def landing(step):
        dr, dc = step
        if dc == 0:
            return row_halo.at[0 if dr < 0 else 1]
        side = col_halo.at[0 if dc < 0 else 1]
        return side.at[pl.ds(1, rows)] if dr == 0 else side.at[0 if dr < 0 else rows + 1]

    def halo_copy(i):
        step = NEAR[i]
        back_i = len(NEAR) - 1 - i
        return push(
            outgoing(step), landing(NEAR[back_i]), near_send.at[i], near_recv.at[back_i],
            neighbour(step),
        )

    local[0].wait()
    pad[:, 1 : rows + 1, EDGE : EDGE + cols, :] = cot[...].astype(F32)
    for m in range(members):
        for r in range(rows):
            edges[0, r, m : m + 1] = cot[m, r, 0:BLOCK].astype(F32)[:1]
            edges[1, r, m : m + 1] = cot[m, r, cols - BLOCK : cols].astype(F32)[BLOCK - 1 :]
    for i in range(len(NEAR)):
        @pl.when(jnp.logical_not(exists(NEAR[i])))
        def _():
            there_ref = landing(NEAR[i])
            there_ref[...] = jnp.zeros(there_ref.shape, there_ref.dtype)

    pl.semaphore_wait(barrier, present + greeted)

    for i in range(len(NEAR)):
        @pl.when(exists(NEAR[i]))
        def _():
            halo_copy(i).start()
    sent = []

    def start(copy):
        copy.start()
        sent.append(copy)

    for o in mem_others:
        start(push(f_hbm.at[:, o], f_got.at[mem], f_send.at[o], f_recv.at[mem], (o, *at)))

    for copy in local[1:]:
        copy.wait()
    eye = one_hot(width, lambda i: i)
    there, back = cell_first(count * members)
    own, mask = cell_masks(count * members)
    wq, wk, wv, wo = (w[...] for w in (wq_v, wk_v, wv_v, wo_v))
    wq_t, wk_t, wv_t = (dot_nt(eye, w).astype(BF16) for w in (wq, wk, wv))
    gain = gain_v[...]
    taps9 = [[taps[i, j : j + 1, :] for j in range(3)] for i in range(3)]

    for i in range(len(NEAR)):
        @pl.when(exists(NEAR[i]))
        def _():
            there_ref = landing(NEAR[i])
            push(
                there_ref, there_ref, near_send.at[i], near_recv.at[i], neighbour(NEAR[i])
            ).wait_recv()
    pad[:, 0, EDGE : EDGE + cols, :] = row_halo[0].astype(F32)
    pad[:, rows + 1, EDGE : EDGE + cols, :] = row_halo[1].astype(F32)
    for side, place in ((0, EDGE - 1), (1, EDGE + cols)):
        for r in range(rows + 2):
            column = col_halo[side, r]
            for m in range(members):
                pad[m, r, place : place + 1, :] = column[m : m + 1]

    seg = min(cells, cols)

    def segments(j):
        for s in range(cells // seg):
            cell = j * cells + s * seg
            yield s * seg, cell // cols, cell % cols

    for j in range(count):
        for first, r, c in segments(j):
            for m in range(members):
                wins = [pad[m, 2 - i + r, c : c + seg + 2 * EDGE, :] for i in range(3)]
                cols3 = [sum(taps9[i][k] * wins[i] for i in range(3)) for k in range(3)]
                summed = sum(
                    cols3[k][EDGE + 1 - k : EDGE + 1 - k + seg] for k in range(3)
                )
                gm_src[m, j, first : first + seg, :] = summed.astype(BF16)

        @pl.when(mem != j)
        def _():
            push(gm_src.at[:, j], gm_got.at[mem], gm_send.at[j], gm_recv.at[mem], (j, *at)).start()

        @pl.when(mem == j)
        def _():
            gm_got[j] = gm_src[:, j]

    for o in mem_others:
        push(f_hbm.at[:, o], f_got.at[o], f_send.at[o], f_recv.at[o], (o, *at)).wait_recv()
    blocks = [slice(i, i + BLOCK) for i in range(0, cells, BLOCK)]
    tokens = count * members * BLOCK
    saved = []
    for b in blocks:
        x = f_got[:, :, b, :].reshape(tokens, width).astype(F32)
        mixed, keep = forward_block(
            x, gain, wq_t, wk_t, wv_t, wk, wv, wo, there, back, eye, own, mask
        )
        mx_src[:, :, b, :] = mixed.reshape(count, members, BLOCK, width)
        saved.append(keep)
    for o in mem_others:
        start(push(mx_src.at[o], mx_got.at[:, mem], mx_send.at[o], mx_recv.at[mem], (o, *at)))
    mx_got[:, mem] = mx_src[mem]

    for o in mem_others:
        push(gm_src.at[:, o], gm_got.at[o], gm_send.at[o], gm_recv.at[o], (o, *at)).wait_recv()
    grads = [
        backward_block(gm_got[:, :, b, :].reshape(tokens, width), keep, wo, there, own, mask)
        for b, keep in zip(blocks, saved)
    ]
    gms = jnp.concatenate([x[0] for x in grads], axis=0)
    in_t = jnp.concatenate([keep[5] for keep in saved], axis=1)
    att_t = jnp.concatenate([keep[6] for keep in saved], axis=1)
    wholes = [
        dot_nt(in_t, jnp.concatenate([x[i] for x in grads], axis=1)) for i in (1, 2, 3)
    ] + [dot_nn(att_t, gms)]
    for i, value in enumerate(wholes):
        for k in range(width // unit):
            flat = i * (width // unit) + k
            half, rest = divmod(flat, planes * grid_rows)
            g[half, rest // grid_rows, rest % grid_rows] = value[k * unit : (k + 1) * unit]

    a_src[...] = g[other].astype(BF16)
    first_copy = push(a_src, a_dst, a_send, a_recv, partner)
    first_copy.start()
    gain_sum = jnp.zeros((1, width), F32)
    for b, keep, x in zip(blocks, saved, grads):
        corr, part = input_block(*x[1:], keep, gain, wq, wk, wv, back)
        co_src[:, :, b, :] = corr.reshape(count, members, BLOCK, width)
        gain_sum = gain_sum + part
    first_copy.wait()
    acc1[...] = g[core] + a_dst[...].astype(F32)
    b_src[...] = acc1[...].astype(BF16)
    turns = row_others[::-1] + [row]
    for r in turns:
        for p in plane_others:
            start(push(
                b_src.at[p, r], b_dst.at[me_p, r], b_send.at[p, r], b_recv.at[me_p, r],
                plane_peer(p),
            ))
    for o in mem_others:
        start(push(co_src.at[o], co_got.at[:, mem], co_send.at[o], co_recv.at[mem], (o, *at)))
    co_got[:, mem] = co_src[mem]

    for o in mem_others:
        push(mx_src.at[o], mx_got.at[:, o], mx_send.at[o], mx_recv.at[o], (o, *at)).wait_recv()
    kernel_sum = [[jnp.zeros((8, width), F32) for _ in range(3)] for _ in range(3)]
    for j in range(count):
        for first, r, c in segments(j):
            for m in range(members):
                mx = mx_got[m, j, first : first + seg, :].astype(F32)
                for k in range(3):
                    ahead = EDGE + 1 - k
                    wide = jnp.concatenate(
                        [
                            jnp.zeros((ahead, width), F32), mx,
                            jnp.zeros((2 * EDGE - ahead, width), F32),
                        ],
                        axis=0,
                    )
                    for i in range(3):
                        win = pad[m, 2 - i + r, c : c + seg + 2 * EDGE, :]
                        product = (wide * win).reshape(-1, 8, width)
                        kernel_sum[i][k] = kernel_sum[i][k] + jnp.sum(product, axis=0)
    s_a[core] = jnp.concatenate(
        [gain_sum]
        + [jnp.sum(kernel_sum[i][k], axis=0, keepdims=True) for i in range(3) for k in range(3)]
        + [jnp.zeros((6, width), F32)],
        axis=0,
    )
    start(push(s_a.at[core], s_a.at[core], sa_send, sa_recv, partner))

    for r in turns:
        for p in plane_others:
            push(
                b_src.at[p, r], b_dst.at[p, r], b_send.at[p, r], b_recv.at[p, r], plane_peer(p)
            ).wait_recv()
        whole = acc1[me_p, r]
        for p in plane_others:
            whole = whole + b_dst[p, r].astype(F32)
        if r is not row:
            c_src[r] = whole.astype(BF16)
            start(push(c_src.at[r], c_dst.at[row], c_send.at[r], c_recv.at[row], (mem, r, col)))
    push(s_a.at[other], s_a.at[other], sa_send, sa_recv, partner).wait_recv()
    s_b[me_p] = s_a[0] + s_a[1]
    for p in plane_others:
        start(push(
            s_b.at[me_p], s_b.at[me_p], sb_send.at[p], sb_recv.at[me_p], plane_peer(p)
        ))
    for r in row_others:
        push(c_src.at[r], c_dst.at[r], c_send.at[r], c_recv.at[r], (mem, r, col)).wait_recv()
        whole = whole + c_dst[r].astype(F32)
    ga[core, me_p, row] = (whole * scale).astype(BF16)

    for r in row_others:
        piece = ga.at[core, me_p, row]
        start(push(piece, piece, z_send.at[r], z_recv.at[row], (mem, r, col)))

    def to_partner(p, r):
        piece = ga.at[core, p, r]
        start(push(piece, piece, g_send.at[p, r], g_recv.at[p, r], partner))
        out_ref[core, p, r] = ga[core, p, r].astype(F32)

    def to_plane(r):
        piece = ga.at[core, me_p, r]
        for p in plane_others:
            start(push(piece, piece, p_send.at[p, r], p_recv.at[me_p, r], plane_peer(p)))
        to_partner(me_p, r)

    def from_plane(r):
        for p in plane_others:
            piece = ga.at[core, p, r]
            push(piece, piece, p_send.at[p, r], p_recv.at[p, r], plane_peer(p)).wait_recv()
            to_partner(p, r)

    to_plane(row)
    for p in plane_others:
        push(s_b.at[p], s_b.at[p], sb_send.at[p], sb_recv.at[p], plane_peer(p)).wait_recv()
    s_c[row] = sum(s_b[p] for p in range(planes))
    for r in row_others:
        start(push(s_c.at[row], s_c.at[row], sc_send.at[r], sc_recv.at[row], (mem, r, col)))
    for o in mem_others:
        push(co_src.at[o], co_got.at[:, o], co_send.at[o], co_recv.at[o], (o, *at)).wait_recv()
    gf_ref[...] = (
        cot[...].astype(F32) + co_got[...].reshape(cot.shape).astype(F32)
    ).astype(BF16)

    before = row
    for r in row_others:
        piece = ga.at[core, me_p, r]
        push(piece, piece, z_send.at[r], z_recv.at[r], (mem, r, col)).wait_recv()
        to_plane(r)
        from_plane(before)
        before = r
    from_plane(before)
    for r in row_others:
        push(s_c.at[r], s_c.at[r], sc_send.at[r], sc_recv.at[r], (mem, r, col)).wait_recv()
    small_ref[...] = sum(s_c[r] for r in range(grid_rows)) * scale
    for r in [row] + row_others:
        for p in [me_p] + plane_others:
            piece = ga.at[other, p, r]
            push(piece, piece, g_send.at[p, r], g_recv.at[p, r], partner).wait_recv()
            out_ref[other, p, r] = ga[other, p, r].astype(F32)

    for copy in sent:
        copy.wait_send()
    for i in range(len(NEAR)):
        @pl.when(exists(NEAR[i]))
        def _():
            halo_copy(i).wait_send()
    for j in range(count):
        @pl.when(mem != j)
        def _():
            push(
                gm_src.at[:, j], gm_got.at[mem], gm_send.at[j], gm_recv.at[mem], (j, *at)
            ).wait_send()


def output_kernel(
    gf_in, out_in, small_in, gf, gain, gq, gk, gv, go, taps, taps_v, sems,
):
    copies = [
        pltpu.make_async_copy(out_in.at[i], ref, sems.at[i]) for i, ref in enumerate((gq, gk, gv, go))
    ]
    copies.append(pltpu.make_async_copy(gf_in, gf, sems.at[4]))
    copies.append(pltpu.make_async_copy(small_in.at[pl.ds(0, 1)], gain, sems.at[5]))
    for copy in copies:
        copy.start()
    for i in range(3):
        taps_v[i] = small_in[1 + 3 * i : 4 + 3 * i, :]
    last = pltpu.make_async_copy(taps_v, taps, sems.at[6])
    last.start()
    for copy in copies:
        copy.wait()
    last.wait()


def local(fields, norm_gain, w_query, w_key, w_value, w_out, mix_kernel, cotangent):
    members, rows, cols, width = fields.shape
    count, grid_rows, grid_cols = (lax.axis_size(a) for a in ("mem", "row", "col"))
    cells = rows * cols // count
    planes = count // 2 * grid_cols
    height = 4 * width
    unit = height // (2 * planes * grid_rows)
    tokens = math.prod(fields.shape[:3]) * count * grid_rows * grid_cols
    sems = pltpu.SemaphoreType.DMA
    vmem = pltpu.VMEM
    split = (members, count, cells, width)
    got = (count, members, cells, width)
    square = vmem((width, width), BF16)
    half = (planes, grid_rows, unit, width)
    line = (grid_rows, unit, width)
    small = (16, width)

    def pair(shape):
        return [sems(shape), sems(shape)]

    gf, out, small_sum = pl.pallas_call(
        functools.partial(
            main_kernel, (count, grid_rows, grid_cols), 1.0 / math.sqrt(tokens)
        ),
        out_shape=(
            jax.ShapeDtypeStruct(fields.shape, BF16),
            jax.ShapeDtypeStruct((2,) + half, F32),
            jax.ShapeDtypeStruct(small, F32),
        ),
        in_specs=[HBM_SPEC] * 8,
        out_specs=(VMEM_SPEC,) * 3,
        scratch_shapes=[
            vmem(fields.shape, BF16), vmem((1, width), F32), square, square, square, square,
            vmem((3, 3, width), F32),
            vmem(got, BF16), vmem(split, BF16), vmem(got, BF16), vmem(got, BF16), vmem(split, BF16),
            vmem(got, BF16), vmem(split, BF16),
            vmem((2, members, cols, width), BF16),
            vmem((2, rows, members, width), F32), vmem((2, rows + 2, members, width), F32),
            vmem((members, rows + 2, cols + 2 * EDGE, width), F32),
            vmem((2,) + half, F32), vmem(half, BF16), vmem(half, BF16), vmem(half, F32),
            vmem(half, BF16), vmem(half, BF16), vmem(line, BF16), vmem(line, BF16),
            vmem((2,) + half, BF16),
            vmem((2,) + small, F32), vmem((planes,) + small, F32), vmem((grid_rows,) + small, F32),
            sems((8,)), *pair((len(NEAR),)),
            *pair((count,)), *pair((count,)), *pair((count,)), *pair((count,)),
            *pair(()), *pair((planes, grid_rows)), *pair((grid_rows,)), *pair((grid_rows,)),
            *pair((planes, grid_rows)), *pair((planes, grid_rows)),
            *pair(()), *pair((planes,)), *pair((grid_rows,)),
        ],
        compiler_params=pltpu.CompilerParams(
            collective_id=1, has_side_effects=True, vmem_limit_bytes=56 * 2**20
        ),
    )(
        fields.reshape(split), cotangent, norm_gain.reshape(1, -1),
        w_query, w_key, w_value, w_out, mix_kernel,
    )
    square32 = jax.ShapeDtypeStruct((width, width), F32)
    gf, gain, gq, gk, gv, go, taps = pl.pallas_call(
        output_kernel,
        out_shape=(
            jax.ShapeDtypeStruct(fields.shape, BF16), jax.ShapeDtypeStruct((1, width), F32),
            square32, square32, square32, square32,
            jax.ShapeDtypeStruct((3, 3, width), F32),
        ),
        in_specs=[VMEM_SPEC] * 3,
        out_specs=(HBM_SPEC,) * 7,
        scratch_shapes=[vmem((3, 3, width), F32), sems((7,))],
        compiler_params=pltpu.CompilerParams(vmem_limit_bytes=16 * 2**20),
    )(gf, out.reshape(4, width, width), small_sum)
    return (gf, gain.reshape(-1), gq, gk, gv, go, taps)


def solution(mesh):
    tile = P("mem", "row", "col", None)
    in_specs = (tile, P(), P(), P(), P(), P(), P(), tile)
    out_specs = (tile, P(), P(), P(), P(), P(), P())
    return jax.shard_map(local, mesh=mesh, in_specs=in_specs, out_specs=out_specs, check_vma=False)
```

time: 64.5 us -> 44 us (0.68)
  Pallas kernels: 54 us -> 40.2 us
  local copies, waits for them, and re-layouts: 7.08 us -> 2.88 us
  other arithmetic: 2.3 us -> 0 us
    pallas_call x4 -> x2, Pallas kernels: 54 us -> 40.2 us  [the longest x1 39.1 us: local(): pl.pallas_call(functools.partial(main_kernel, (count, grid_rows, grid_col...]
    slice x4 -> x0, local copies, waits for them, and re-layouts: 2.45 us -> none  [the longest x1 0.98 us: local(): w = [total[i * width:(i + 1) * width] for i in range(4)]]
    reduce_sum x1 -> x0, other arithmetic: 1.5 us -> none  [local(): terms = [jnp.sum(s * mixed, axis=(0, 1, 2))[None] for s in shifts]]
    reshape x2 -> x0, local copies, waits for them, and re-layouts: 1.33 us -> none  [the longest x1 0.72 us: local(): mix_kernel.reshape(9, width)]
    convert_element_type x1 -> x0, other arithmetic: 0.78 us -> none  [local(): (cotangent.astype(F32) + corr.reshape(fields.shape).astype(F32)).astype(B...]
    unnamed x18 -> x6, local copies, waits for them, and re-layouts: 3.24 us -> 2.88 us
where the time goes in v1:
time: 44 us; the launch traced here: 43.7 us
  Pallas kernels  40.2 us (91%)
  local copies, waits for them, and re-layouts  2.88 us (7%)
  between operations  0.65 us (1%)
    pallas_call x1, Pallas kernels, local(): pl.pallas_call(functools.partial(main_kernel, (count, grid_rows, grid_col...  39.1 us
    unnamed x6, local copies, waits for them, and re-layouts  2.88 us
    pallas_call x1, Pallas kernels, local(): pl.pallas_call(output_kernel, out_shape=(jax.ShapeDtypeStruct(fields.shap...  1.11 us

profile of v1, /device:TPU:0, one launch (start us, length us, event | category | flops | bytes accessed | tf_op | source)
XLA Modules:
  0.0 43.7 jit_solution(14748878590259846520)
XLA Ops:
  0.6 39.1 %shard_map.135 = (bf16[4,4,32,256]{3,2,1,0:T(8,128)(2,1)}, f32[2,4,4,32,256]{4,3,2,1,0:T(8,128)}, f32[16,256]{1,0:T(8,128)}) custom-call(bf16[4,4,32,256]{3,2,1,0:T(8,128)(2,1)} %f_hbm.1, bf16[4,4,32,256]{3,2,1,0:T(8,128)(2,1)} %cot_hbm.1, f32[1,256]{1,0:T(1,128)} %bitcast.4, bf16[256,256]{1,0:T(8,128)(2,1)} %wq_hbm.1, bf16[256,256]{1,0:T(8,128)(2,1)} %wk_hbm.1, ...), custom_call_target="tpu_custom_call" | custom-call | tf_op jit(solution)/shard_map/pallas_call | solution.py:559
  39.7 0.0 copy-start
  39.7 1.2 %copy-done = f32[2,4,4,32,256]{4,3,2,1,0:T(8,128)S(1)} copy-done((f32[2,4,4,32,256]{4,3,2,1,0:T(8,128)S(1)}, f32[2,4,4,32,256]{4,3,2,1,0:T(8,128)}, u32[]{:S(2)}) %copy-start) | copy-done | bytes 1048600
  40.9 0.0 copy-start.1
  41.0 0.9 %copy-done.1 = bf16[4,4,32,256]{3,2,1,0:T(8,128)(2,1)S(1)} copy-done((bf16[4,4,32,256]{3,2,1,0:T(8,128)(2,1)S(1)}, bf16[4,4,32,256]{3,2,1,0:T(8,128)(2,1)}, u32[]{:S(2)}) %copy-start.1) | copy-done | bytes 262168
  41.9 0.0 copy-start.2
  41.9 0.7 %copy-done.2 = f32[16,256]{1,0:T(8,128)S(1)} copy-done((f32[16,256]{1,0:T(8,128)S(1)}, f32[16,256]{1,0:T(8,128)}, u32[]{:S(2)}) %copy-start.2) | copy-done | bytes 16408
  42.6 1.1 %shard_map.136 = (bf16[4,4,32,256]{3,2,1,0:T(8,128)(2,1)}, f32[1,256]{1,0:T(1,128)}, f32[256,256]{1,0:T(8,128)}, f32[256,256]{1,0:T(8,128)}, f32[256,256]{1,0:T(...) custom-call(bf16[4,4,32,256]{3,2,1,0:T(8,128)(2,1)S(1)} %copy-done.1, f32[4,256,256]{2,1,0:T(8,128)S(1)} %bitcast.3, ...), custom_call_target="tpu_custom_call" | custom-call | tf_op jit(solution)/shard_map/pallas_call | solution.py:596
Async XLA Ops:
  39.7 1.2 %copy-start = (f32[2,4,4,32,256]{4,3,2,1,0:T(8,128)S(1)}, f32[2,4,4,32,256]{4,3,2,1,0:T(8,128)}, u32[]{:S(2)}) copy-start(f32[2,4,4,32,256]{4,3,2,1,0:T(8,128)} %get-tuple-element.18) | copy-start | bytes 3145732
  40.9 0.9 %copy-start.1 = (bf16[4,4,32,256]{3,2,1,0:T(8,128)(2,1)S(1)}, bf16[4,4,32,256]{3,2,1,0:T(8,128)(2,1)}, u32[]{:S(2)}) copy-start(bf16[4,4,32,256]{3,2,1,0:T(8,128)(2,1)} %get-tuple-element.17.gf_in) | copy-start | bytes 786436
  41.9 0.7 %copy-start.2 = (f32[16,256]{1,0:T(8,128)S(1)}, f32[16,256]{1,0:T(8,128)}, u32[]{:S(2)}) copy-start(f32[16,256]{1,0:T(8,128)} %get-tuple-element.19.small_in) | copy-start | bytes 49156

commit v2 on v1

--- a/solution.py
+++ b/solution.py
@@ -586,12 +586,15 @@
             *pair(()), *pair((planes,)), *pair((grid_rows,)),
         ],
         compiler_params=pltpu.CompilerParams(
-            collective_id=1, has_side_effects=True, vmem_limit_bytes=56 * 2**20
+            collective_id=1, has_side_effects=True, vmem_limit_bytes=24 * 2**20
         ),
-    )(
-        fields.reshape(split), cotangent, norm_gain.reshape(1, -1),
-        w_query, w_key, w_value, w_out, mix_kernel,
-    )
+    )(*(
+        pltpu.with_memory_space_constraint(x, pltpu.HBM)
+        for x in (
+            fields.reshape(split), cotangent, norm_gain.reshape(1, -1),
+            w_query, w_key, w_value, w_out, mix_kernel,
+        )
+    ))
     square32 = jax.ShapeDtypeStruct((width, width), F32)
     gf, gain, gq, gk, gv, go, taps = pl.pallas_call(
         output_kernel,

time: 44 us -> 39.9 us (0.907)
  local copies, waits for them, and re-layouts: 2.88 us -> 0 us
  Pallas kernels: 40.2 us -> 39.1 us
    unnamed x6 -> x0, local copies, waits for them, and re-layouts: 2.88 us -> none
    pallas_call x1, Pallas kernels: 39.1 us -> 38 us  [local(): pl.pallas_call(functools.partial(main_kernel, (count, grid_rows, grid_col...]
where the time goes in v2:
time: 39.9 us; the launch traced here: 39.8 us
  Pallas kernels  39.1 us (98%)
  between operations  0.64 us (2%)
    pallas_call x1, Pallas kernels, local(): pl.pallas_call(functools.partial(main_kernel, (count, grid_rows, grid_col...  38 us
    pallas_call x1, Pallas kernels, local(): pl.pallas_call(output_kernel, out_shape=(jax.ShapeDtypeStruct(fields.shap...  1.11 us

profile of v2, /device:TPU:0, one launch (start us, length us, event | category | flops | bytes accessed | tf_op | source)
XLA Modules:
  0.0 39.8 jit_solution(3597243420963057076)
XLA Ops:
  0.6 38.0 %shard_map.135 = (bf16[4,4,32,256]{3,2,1,0:T(8,128)(2,1)S(1)}, f32[2,4,4,32,256]{4,3,2,1,0:T(8,128)S(1)}, f32[16,256]{1,0:T(8,128)S(1)}) custom-call(bf16[4,4,32,256]{3,2,1,0:T(8,128)(2,1)} %f_hbm.1, bf16[4,4,32,256]{3,2,1,0:T(8,128)(2,1)} %cot_hbm.1, f32[1,256]{1,0:T(1,128)} %bitcast.4, bf16[256,256]{1,0:T(8,128)(2,1)} %wq_hbm.1, bf16[256,256]{1,0:T(8,128)(2,1)} %wk_hbm.1, ...), custom_call_target="tpu_custom_call" | custom-call | tf_op jit(solution)/shard_map/pallas_call | solution.py:559
  38.6 1.1 %shard_map.136 = (bf16[4,4,32,256]{3,2,1,0:T(8,128)(2,1)}, f32[1,256]{1,0:T(1,128)}, f32[256,256]{1,0:T(8,128)}, f32[256,256]{1,0:T(8,128)}, f32[256,256]{1,0:T(...) custom-call(bf16[4,4,32,256]{3,2,1,0:T(8,128)(2,1)S(1)} %get-tuple-element.17.gf_in, f32[4,256,256]{2,1,0:T(8,128)S(1)} %bitcast.3, ...), custom_call_target="tpu_custom_call" | custom-call | tf_op jit(solution)/shard_map/pallas_call | solution.py:599

commit v3 on v2

--- a/solution.py
+++ b/solution.py
@@ -95,19 +95,28 @@
     ).astype(BF16)
 
 
-def back_group(prob, vals, q_t, ga_t, k_t, own, mask):
+def back_values(prob, ga_t, mask):
+    dim = ga_t.shape[0] // HEADS
+    return jnp.concatenate(
+        [
+            dot_nt(ga_t[h * dim : (h + 1) * dim], spread(prob[h].astype(BF16), mask))
+            for h in range(HEADS)
+        ],
+        axis=0,
+    ).astype(BF16)
+
+
+def back_scores(prob, vals, q_t, ga_t, k_t, own, mask):
     dim = vals.shape[1] // HEADS
     grad_prob = own_cells(vals, ga_t, own)
     inner = jnp.sum(prob * grad_prob, axis=1, keepdims=True)
     grad_score = prob * (grad_prob - inner) * (1.0 / math.sqrt(dim))
-    outs = ([], [], [])
+    outs = ([], [])
     for h in range(HEADS):
         hs = slice(h * dim, (h + 1) * dim)
         gs = spread(grad_score[h].astype(BF16), mask)
-        pb = spread(prob[h].astype(BF16), mask)
         outs[0].append(dot_nn(k_t[hs], gs))
         outs[1].append(dot_nt(q_t[hs], gs))
-        outs[2].append(dot_nt(ga_t[hs], pb))
     return tuple(jnp.concatenate(o, axis=0).astype(BF16) for o in outs)
 
 
@@ -138,16 +147,25 @@
     return mixed, (inv, normed, vals, q_t, k_t, in_t, att_t, probs)
 
 
-def backward_block(gm, saved, wo, there, own, mask):
-    inv, normed, vals, q_t, k_t, in_t, att_t, probs = saved
-    tokens = gm.shape[0]
+def early_block(gm, saved, wo, there, mask):
+    probs = saved[-1]
     gm = dot_nn(there, gm).astype(BF16)
     ga_t = dot_nt(wo, gm).astype(BF16)
+    cuts = groups_of(gm.shape[0], gm.shape[0] // BLOCK)
+    gv_t = jnp.concatenate(
+        [back_values(prob, ga_t[:, s], mask) for s, prob in zip(cuts, probs)], axis=1
+    )
+    return gm, ga_t, gv_t
+
+
+def late_block(ga_t, saved, own, mask):
+    inv, normed, vals, q_t, k_t, in_t, att_t, probs = saved
+    tokens = vals.shape[0]
     parts = [
-        back_group(prob, vals[s], q_t[:, s], ga_t[:, s], k_t[:, s], own, mask)
+        back_scores(prob, vals[s], q_t[:, s], ga_t[:, s], k_t[:, s], own, mask)
         for s, prob in zip(groups_of(tokens, tokens // BLOCK), probs)
     ]
-    return (gm,) + tuple(jnp.concatenate(p, axis=1) for p in zip(*parts))
+    return tuple(jnp.concatenate(p, axis=1) for p in zip(*parts))
 
 
 def input_block(gq_t, gk_t, gv_t, saved, gain, wq, wk, wv, back):
@@ -172,9 +190,9 @@
     gf_ref, out_ref, small_ref,
     cot, gain_v, wq_v, wk_v, wv_v, wo_v, taps, f_got, gm_src, gm_got, mx_src, mx_got,
     co_src, co_got, row_halo, edges, col_halo, pad,
-    g, a_src, a_dst, acc1, b_src, b_dst, c_src, c_dst, ga, s_a, s_b, s_c,
+    g, a_src, a_dst, acc, b_src, b_dst, c_all, ga, s_a, s_b, s_c,
     load, near_send, near_recv, f_send, f_recv, gm_send, gm_recv, mx_send, mx_recv,
-    co_send, co_recv, a_send, a_recv, b_send, b_recv, c_send, c_recv, z_send, z_recv,
+    co_send, co_recv, a_send, a_recv, b_send, b_recv, c_send, c_recv,
     p_send, p_recv, g_send, g_recv,
     sa_send, sa_recv, sb_send, sb_recv, sc_send, sc_recv,
 ):
@@ -182,7 +200,7 @@
     members, rows, cols, width = cot.shape
     cells = f_got.shape[2]
     planes = count // 2 * grid_cols
-    unit = g.shape[3]
+    subs, unit = g.shape[3:5]
     mem, row, col = (lax.axis_index(a) for a in ("mem", "row", "col"))
     at = (row, col)
     core, chip = lax.rem(mem, 2), lax.div(mem, 2)
@@ -193,13 +211,16 @@
     def plane_peer(p):
         return (lax.div(p, grid_cols) * 2 + core, row, lax.rem(p, grid_cols))
 
-    mem_others = [lax.rem(mem + k, count) for k in range(1, count)]
+    mem_others = [
+        lax.rem(chip + k, count // 2) * 2 + c for k in range(1, count // 2) for c in (core, other)
+    ] + [partner[0]]
     plane_others = [lax.rem(me_p + k, planes) for k in range(1, planes)]
     step_z = 1 - 2 * lax.div(row * 2, grid_rows)
     row_others = [
         lax.rem(row + step_z * k + grid_rows, grid_rows) for k in range(1, grid_rows)
     ]
 
+    far_rows = row_others[::-1]
     local = [
         pltpu.make_async_copy(cot_hbm, cot, load.at[0]),
         pltpu.make_async_copy(taps_hbm, taps, load.at[1]),
@@ -270,33 +291,50 @@
             neighbour(step),
         )
 
+    straight = [i for i in range(len(NEAR)) if NEAR[i][1] == 0]
+    sideways = [i for i in range(len(NEAR)) if NEAR[i][1] != 0]
+    sent = []
+
+    def start(copy):
+        copy.start()
+        sent.append(copy)
+
+    def send_halo(steps):
+        for i in steps:
+            @pl.when(exists(NEAR[i]))
+            def _():
+                halo_copy(i).start()
+
+    def wait_halo(steps):
+        for i in steps:
+            @pl.when(exists(NEAR[i]))
+            def _():
+                there_ref = landing(NEAR[i])
+                push(
+                    there_ref, there_ref, near_send.at[i], near_recv.at[i], neighbour(NEAR[i])
+                ).wait_recv()
+
+    for i in range(len(NEAR)):
+        @pl.when(jnp.logical_not(exists(NEAR[i])))
+        def _():
+            there_ref = landing(NEAR[i])
+            there_ref[...] = jnp.zeros(there_ref.shape, there_ref.dtype)
+    blocks = [slice(i, i + BLOCK) for i in range(0, cells, BLOCK)]
+
     local[0].wait()
     pad[:, 1 : rows + 1, EDGE : EDGE + cols, :] = cot[...].astype(F32)
     for m in range(members):
         for r in range(rows):
             edges[0, r, m : m + 1] = cot[m, r, 0:BLOCK].astype(F32)[:1]
             edges[1, r, m : m + 1] = cot[m, r, cols - BLOCK : cols].astype(F32)[BLOCK - 1 :]
-    for i in range(len(NEAR)):
-        @pl.when(jnp.logical_not(exists(NEAR[i])))
-        def _():
-            there_ref = landing(NEAR[i])
-            there_ref[...] = jnp.zeros(there_ref.shape, there_ref.dtype)
-
     pl.semaphore_wait(barrier, present + greeted)
-
-    for i in range(len(NEAR)):
-        @pl.when(exists(NEAR[i]))
-        def _():
-            halo_copy(i).start()
-    sent = []
-
-    def start(copy):
-        copy.start()
-        sent.append(copy)
-
-    for o in mem_others:
-        start(push(f_hbm.at[:, o], f_got.at[mem], f_send.at[o], f_recv.at[mem], (o, *at)))
-
+    send_halo(sideways)
+    send_halo(straight)
+    for i, b in enumerate(blocks):
+        for o in mem_others:
+            start(push(
+                f_hbm.at[:, o, b], f_got.at[mem, :, b], f_send.at[o, i], f_recv.at[mem, i], (o, *at)
+            ))
     for copy in local[1:]:
         copy.wait()
     eye = one_hot(width, lambda i: i)
@@ -307,15 +345,7 @@
     gain = gain_v[...]
     taps9 = [[taps[i, j : j + 1, :] for j in range(3)] for i in range(3)]
 
-    for i in range(len(NEAR)):
-        @pl.when(exists(NEAR[i]))
-        def _():
-            there_ref = landing(NEAR[i])
-            push(
-                there_ref, there_ref, near_send.at[i], near_recv.at[i], neighbour(NEAR[i])
-            ).wait_recv()
-    pad[:, 0, EDGE : EDGE + cols, :] = row_halo[0].astype(F32)
-    pad[:, rows + 1, EDGE : EDGE + cols, :] = row_halo[1].astype(F32)
+    wait_halo(sideways)
     for side, place in ((0, EDGE - 1), (1, EDGE + cols)):
         for r in range(rows + 2):
             column = col_halo[side, r]
@@ -329,7 +359,7 @@
             cell = j * cells + s * seg
             yield s * seg, cell // cols, cell % cols
 
-    for j in range(count):
+    def send_mixed_gradient(j):
         for first, r, c in segments(j):
             for m in range(members):
                 wins = [pad[m, 2 - i + r, c : c + seg + 2 * EDGE, :] for i in range(3)]
@@ -347,64 +377,159 @@
         def _():
             gm_got[j] = gm_src[:, j]
 
-    for o in mem_others:
-        push(f_hbm.at[:, o], f_got.at[o], f_send.at[o], f_recv.at[o], (o, *at)).wait_recv()
-    blocks = [slice(i, i + BLOCK) for i in range(0, cells, BLOCK)]
+    def inner(j):
+        return all(0 < r < rows - 1 for _, r, _ in segments(j))
+
+    for j in range(count):
+        if inner(j):
+            send_mixed_gradient(j)
+    wait_halo(straight)
+    pad[:, 0, EDGE : EDGE + cols, :] = row_halo[0].astype(F32)
+    pad[:, rows + 1, EDGE : EDGE + cols, :] = row_halo[1].astype(F32)
+    for j in range(count):
+        if not inner(j):
+            send_mixed_gradient(j)
+
     tokens = count * members * BLOCK
     saved = []
-    for b in blocks:
+    for i, b in enumerate(blocks):
+        for o in mem_others:
+            push(
+                f_hbm.at[:, o, b], f_got.at[o, :, b], f_send.at[o, i], f_recv.at[o, i], (o, *at)
+            ).wait_recv()
         x = f_got[:, :, b, :].reshape(tokens, width).astype(F32)
         mixed, keep = forward_block(
             x, gain, wq_t, wk_t, wv_t, wk, wv, wo, there, back, eye, own, mask
         )
         mx_src[:, :, b, :] = mixed.reshape(count, members, BLOCK, width)
         saved.append(keep)
-    for o in mem_others:
-        start(push(mx_src.at[o], mx_got.at[:, mem], mx_send.at[o], mx_recv.at[mem], (o, *at)))
+    for i, b in enumerate(blocks):
+        for o in mem_others:
+            start(push(
+                mx_src.at[o, :, b], mx_got.at[:, mem, b], mx_send.at[o, i], mx_recv.at[mem, i],
+                (o, *at),
+            ))
     mx_got[:, mem] = mx_src[mem]
 
     for o in mem_others:
         push(gm_src.at[:, o], gm_got.at[o], gm_send.at[o], gm_recv.at[o], (o, *at)).wait_recv()
-    grads = [
-        backward_block(gm_got[:, :, b, :].reshape(tokens, width), keep, wo, there, own, mask)
+    def store(chunk, values):
+        for half, value in enumerate(values):
+            for k in range(width // unit):
+                g[chunk, half, k // subs, k % subs] = value[k * unit : (k + 1) * unit]
+
+    def to_core(chunk):
+        a_src[chunk] = g[chunk, other].astype(BF16)
+        start(push(
+            a_src.at[chunk], a_dst.at[chunk], a_send.at[chunk], a_recv.at[chunk], partner
+        ))
+
+    def to_owner(chunk):
+        push(
+            a_src.at[chunk], a_dst.at[chunk], a_send.at[chunk], a_recv.at[chunk], partner
+        ).wait_recv()
+        acc[chunk] = g[chunk, core] + a_dst[chunk].astype(F32)
+        b_src[chunk] = acc[chunk].astype(BF16)
+        for s in range(subs):
+            for p in plane_others:
+                start(push(
+                    b_src.at[chunk, p, s], b_dst.at[chunk, me_p, s],
+                    b_send.at[chunk, p, s], b_recv.at[chunk, me_p, s], plane_peer(p),
+                ))
+
+    def to_rows(chunk):
+        for s in range(subs):
+            for p in plane_others:
+                push(
+                    b_src.at[chunk, p, s], b_dst.at[chunk, p, s],
+                    b_send.at[chunk, p, s], b_recv.at[chunk, p, s], plane_peer(p),
+                ).wait_recv()
+            whole = acc[chunk, me_p, s]
+            for p in plane_others:
+                whole = whole + b_dst[chunk, p, s].astype(F32)
+            c_all[chunk, s, row] = whole.astype(BF16)
+            for r in far_rows:
+                piece = c_all.at[chunk, s, row]
+                start(push(
+                    piece, piece, c_send.at[chunk, s, r], c_recv.at[chunk, s, row], (mem, r, col)
+                ))
+
+    def to_partner(chunk, p, s):
+        piece = ga.at[chunk, core, p, s]
+        start(push(
+            piece, piece, g_send.at[chunk, p, s], g_recv.at[chunk, p, s], partner
+        ))
+        out_ref[chunk, core, p, s] = ga[chunk, core, p, s].astype(F32)
+
+    def to_plane(chunk):
+        for s in range(subs):
+            for r in row_others:
+                piece = c_all.at[chunk, s, r]
+                push(
+                    piece, piece, c_send.at[chunk, s, r], c_recv.at[chunk, s, r], (mem, r, col)
+                ).wait_recv()
+            whole = sum(c_all[chunk, s, r].astype(F32) for r in range(grid_rows))
+            ga[chunk, core, me_p, s] = (whole * scale).astype(BF16)
+            piece = ga.at[chunk, core, me_p, s]
+            for p in plane_others:
+                start(push(
+                    piece, piece, p_send.at[chunk, p, s], p_recv.at[chunk, me_p, s], plane_peer(p)
+                ))
+            to_partner(chunk, me_p, s)
+
+    def from_plane(chunk):
+        for s in range(subs):
+            for p in plane_others:
+                piece = ga.at[chunk, core, p, s]
+                push(
+                    piece, piece, p_send.at[chunk, p, s], p_recv.at[chunk, p, s], plane_peer(p)
+                ).wait_recv()
+                to_partner(chunk, p, s)
+
+    def from_partner(chunk):
+        for s in range(subs):
+            for p in [me_p] + plane_others:
+                piece = ga.at[chunk, other, p, s]
+                push(
+                    piece, piece, g_send.at[chunk, p, s], g_recv.at[chunk, p, s], partner
+                ).wait_recv()
+                out_ref[chunk, other, p, s] = ga[chunk, other, p, s].astype(F32)
+
+    early = [
+        early_block(gm_got[:, :, b, :].reshape(tokens, width), keep, wo, there, mask)
         for b, keep in zip(blocks, saved)
     ]
-    gms = jnp.concatenate([x[0] for x in grads], axis=0)
     in_t = jnp.concatenate([keep[5] for keep in saved], axis=1)
     att_t = jnp.concatenate([keep[6] for keep in saved], axis=1)
-    wholes = [
-        dot_nt(in_t, jnp.concatenate([x[i] for x in grads], axis=1)) for i in (1, 2, 3)
-    ] + [dot_nn(att_t, gms)]
-    for i, value in enumerate(wholes):
-        for k in range(width // unit):
-            flat = i * (width // unit) + k
-            half, rest = divmod(flat, planes * grid_rows)
-            g[half, rest // grid_rows, rest % grid_rows] = value[k * unit : (k + 1) * unit]
-
-    a_src[...] = g[other].astype(BF16)
-    first_copy = push(a_src, a_dst, a_send, a_recv, partner)
-    first_copy.start()
+    store(0, (
+        dot_nt(in_t, jnp.concatenate([x[2] for x in early], axis=1)),
+        dot_nn(att_t, jnp.concatenate([x[0] for x in early], axis=0)),
+    ))
+    to_core(0)
+    late = []
+    for i, (x, keep) in enumerate(zip(early, saved)):
+        late.append(late_block(x[1], keep, own, mask))
+        if i == 0:
+            to_owner(0)
+    store(1, tuple(
+        dot_nt(in_t, jnp.concatenate([x[i] for x in late], axis=1)) for i in range(2)
+    ))
+    to_core(1)
     gain_sum = jnp.zeros((1, width), F32)
-    for b, keep, x in zip(blocks, saved, grads):
-        corr, part = input_block(*x[1:], keep, gain, wq, wk, wv, back)
+    for b, keep, x, y in zip(blocks, saved, early, late):
+        corr, part = input_block(*y, x[2], keep, gain, wq, wk, wv, back)
         co_src[:, :, b, :] = corr.reshape(count, members, BLOCK, width)
         gain_sum = gain_sum + part
-    first_copy.wait()
-    acc1[...] = g[core] + a_dst[...].astype(F32)
-    b_src[...] = acc1[...].astype(BF16)
-    turns = row_others[::-1] + [row]
-    for r in turns:
-        for p in plane_others:
-            start(push(
-                b_src.at[p, r], b_dst.at[me_p, r], b_send.at[p, r], b_recv.at[me_p, r],
-                plane_peer(p),
-            ))
+    to_owner(1)
     for o in mem_others:
         start(push(co_src.at[o], co_got.at[:, mem], co_send.at[o], co_recv.at[mem], (o, *at)))
     co_got[:, mem] = co_src[mem]
-
-    for o in mem_others:
-        push(mx_src.at[o], mx_got.at[:, o], mx_send.at[o], mx_recv.at[o], (o, *at)).wait_recv()
+    for i, b in enumerate(blocks):
+        for o in mem_others:
+            push(
+                mx_src.at[o, :, b], mx_got.at[:, o, b], mx_send.at[o, i], mx_recv.at[o, i],
+                (o, *at),
+            ).wait_recv()
     kernel_sum = [[jnp.zeros((8, width), F32) for _ in range(3)] for _ in range(3)]
     for j in range(count):
         for first, r, c in segments(j):
@@ -430,78 +555,34 @@
         axis=0,
     )
     start(push(s_a.at[core], s_a.at[core], sa_send, sa_recv, partner))
-
-    for r in turns:
-        for p in plane_others:
-            push(
-                b_src.at[p, r], b_dst.at[p, r], b_send.at[p, r], b_recv.at[p, r], plane_peer(p)
-            ).wait_recv()
-        whole = acc1[me_p, r]
-        for p in plane_others:
-            whole = whole + b_dst[p, r].astype(F32)
-        if r is not row:
-            c_src[r] = whole.astype(BF16)
-            start(push(c_src.at[r], c_dst.at[row], c_send.at[r], c_recv.at[row], (mem, r, col)))
+    to_rows(0)
+
     push(s_a.at[other], s_a.at[other], sa_send, sa_recv, partner).wait_recv()
     s_b[me_p] = s_a[0] + s_a[1]
     for p in plane_others:
         start(push(
             s_b.at[me_p], s_b.at[me_p], sb_send.at[p], sb_recv.at[me_p], plane_peer(p)
         ))
-    for r in row_others:
-        push(c_src.at[r], c_dst.at[r], c_send.at[r], c_recv.at[r], (mem, r, col)).wait_recv()
-        whole = whole + c_dst[r].astype(F32)
-    ga[core, me_p, row] = (whole * scale).astype(BF16)
-
-    for r in row_others:
-        piece = ga.at[core, me_p, row]
-        start(push(piece, piece, z_send.at[r], z_recv.at[row], (mem, r, col)))
-
-    def to_partner(p, r):
-        piece = ga.at[core, p, r]
-        start(push(piece, piece, g_send.at[p, r], g_recv.at[p, r], partner))
-        out_ref[core, p, r] = ga[core, p, r].astype(F32)
-
-    def to_plane(r):
-        piece = ga.at[core, me_p, r]
-        for p in plane_others:
-            start(push(piece, piece, p_send.at[p, r], p_recv.at[me_p, r], plane_peer(p)))
-        to_partner(me_p, r)
-
-    def from_plane(r):
-        for p in plane_others:
-            piece = ga.at[core, p, r]
-            push(piece, piece, p_send.at[p, r], p_recv.at[p, r], plane_peer(p)).wait_recv()
-            to_partner(p, r)
-
-    to_plane(row)
+    to_rows(1)
+    to_plane(0)
     for p in plane_others:
         push(s_b.at[p], s_b.at[p], sb_send.at[p], sb_recv.at[p], plane_peer(p)).wait_recv()
     s_c[row] = sum(s_b[p] for p in range(planes))
-    for r in row_others:
+    for r in far_rows:
         start(push(s_c.at[row], s_c.at[row], sc_send.at[r], sc_recv.at[row], (mem, r, col)))
+    to_plane(1)
     for o in mem_others:
         push(co_src.at[o], co_got.at[:, o], co_send.at[o], co_recv.at[o], (o, *at)).wait_recv()
     gf_ref[...] = (
         cot[...].astype(F32) + co_got[...].reshape(cot.shape).astype(F32)
     ).astype(BF16)
-
-    before = row
-    for r in row_others:
-        piece = ga.at[core, me_p, r]
-        push(piece, piece, z_send.at[r], z_recv.at[r], (mem, r, col)).wait_recv()
-        to_plane(r)
-        from_plane(before)
-        before = r
-    from_plane(before)
+    from_plane(0)
     for r in row_others:
         push(s_c.at[r], s_c.at[r], sc_send.at[r], sc_recv.at[r], (mem, r, col)).wait_recv()
     small_ref[...] = sum(s_c[r] for r in range(grid_rows)) * scale
-    for r in [row] + row_others:
-        for p in [me_p] + plane_others:
-            piece = ga.at[other, p, r]
-            push(piece, piece, g_send.at[p, r], g_recv.at[p, r], partner).wait_recv()
-            out_ref[other, p, r] = ga[other, p, r].astype(F32)
+    from_plane(1)
+    from_partner(0)
+    from_partner(1)
 
     for copy in sent:
         copy.wait_send()
@@ -521,7 +602,7 @@
     gf_in, out_in, small_in, gf, gain, gq, gk, gv, go, taps, taps_v, sems,
 ):
     copies = [
-        pltpu.make_async_copy(out_in.at[i], ref, sems.at[i]) for i, ref in enumerate((gq, gk, gv, go))
+        pltpu.make_async_copy(out_in.at[i], ref, sems.at[i]) for i, ref in enumerate((gv, go, gq, gk))
     ]
     copies.append(pltpu.make_async_copy(gf_in, gf, sems.at[4]))
     copies.append(pltpu.make_async_copy(small_in.at[pl.ds(0, 1)], gain, sems.at[5]))
@@ -541,17 +622,18 @@
     count, grid_rows, grid_cols = (lax.axis_size(a) for a in ("mem", "row", "col"))
     cells = rows * cols // count
     planes = count // 2 * grid_cols
-    height = 4 * width
-    unit = height // (2 * planes * grid_rows)
+    subs = 2
+    unit = width // (planes * subs)
     tokens = math.prod(fields.shape[:3]) * count * grid_rows * grid_cols
     sems = pltpu.SemaphoreType.DMA
     vmem = pltpu.VMEM
     split = (members, count, cells, width)
     got = (count, members, cells, width)
     square = vmem((width, width), BF16)
-    half = (planes, grid_rows, unit, width)
-    line = (grid_rows, unit, width)
+    half = (2, planes, subs, unit, width)
+    full = (2,) + half
     small = (16, width)
+    steps = cells // BLOCK
 
     def pair(shape):
         return [sems(shape), sems(shape)]
@@ -562,7 +644,7 @@
         ),
         out_shape=(
             jax.ShapeDtypeStruct(fields.shape, BF16),
-            jax.ShapeDtypeStruct((2,) + half, F32),
+            jax.ShapeDtypeStruct(full, F32),
             jax.ShapeDtypeStruct(small, F32),
         ),
         in_specs=[HBM_SPEC] * 8,
@@ -575,14 +657,14 @@
             vmem((2, members, cols, width), BF16),
             vmem((2, rows, members, width), F32), vmem((2, rows + 2, members, width), F32),
             vmem((members, rows + 2, cols + 2 * EDGE, width), F32),
-            vmem((2,) + half, F32), vmem(half, BF16), vmem(half, BF16), vmem(half, F32),
-            vmem(half, BF16), vmem(half, BF16), vmem(line, BF16), vmem(line, BF16),
-            vmem((2,) + half, BF16),
+            vmem(full, F32), vmem(half, BF16), vmem(half, BF16), vmem(half, F32),
+            vmem(half, BF16), vmem(half, BF16), vmem((2, subs, grid_rows, unit, width), BF16),
+            vmem(full, BF16),
             vmem((2,) + small, F32), vmem((planes,) + small, F32), vmem((grid_rows,) + small, F32),
             sems((8,)), *pair((len(NEAR),)),
-            *pair((count,)), *pair((count,)), *pair((count,)), *pair((count,)),
-            *pair(()), *pair((planes, grid_rows)), *pair((grid_rows,)), *pair((grid_rows,)),
-            *pair((planes, grid_rows)), *pair((planes, grid_rows)),
+            *pair((count, steps)), *pair((count,)), *pair((count, steps)), *pair((count,)),
+            *pair((2,)), *pair((2, planes, subs)), *pair((2, subs, grid_rows)),
+            *pair((2, planes, subs)), *pair((2, planes, subs)),
             *pair(()), *pair((planes,)), *pair((grid_rows,)),
         ],
         compiler_params=pltpu.CompilerParams(

time: 39.9 us -> 36.5 us (0.915)
  Pallas kernels: 39.1 us -> 35.7 us
    pallas_call x1, Pallas kernels: 38 us -> 34.5 us  [local(): pl.pallas_call(functools.partial(main_kernel, (count, grid_rows, grid_col...]
where the time goes in v3:
time: 36.5 us; the launch traced here: 36.3 us
  Pallas kernels  35.7 us (98%)
  between operations  0.64 us (2%)
    pallas_call x1, Pallas kernels, local(): pl.pallas_call(functools.partial(main_kernel, (count, grid_rows, grid_col...  34.5 us
    pallas_call x1, Pallas kernels, local(): pl.pallas_call(output_kernel, out_shape=(jax.ShapeDtypeStruct(fields.shap...  1.11 us

profile of v3, /device:TPU:0, one launch (start us, length us, event | category | flops | bytes accessed | tf_op | source)
XLA Modules:
  0.0 36.3 jit_solution(18230653935449098446)
XLA Ops:
  0.6 34.5 %shard_map.135 = (bf16[4,4,32,256]{3,2,1,0:T(8,128)(2,1)S(1)}, f32[2,2,4,2,32,256]{5,4,3,2,1,0:T(8,128)S(1)}, f32[16,256]{1,0:T(8,128)S(1)}) custom-call(bf16[4,4,32,256]{3,2,1,0:T(8,128)(2,1)} %f_hbm.1, bf16[4,4,32,256]{3,2,1,0:T(8,128)(2,1)} %cot_hbm.1, f32[1,256]{1,0:T(1,128)} %bitcast.4, bf16[256,256]{1,0:T(8,128)(2,1)} %wq_hbm.1, ...), custom_call_target="tpu_custom_call" | custom-call | tf_op jit(solution)/shard_map/pallas_call | solution.py:641
  35.2 1.1 %shard_map.136 = (bf16[4,4,32,256]{3,2,1,0:T(8,128)(2,1)}, f32[1,256]{1,0:T(1,128)}, f32[256,256]{1,0:T(8,128)}, f32[256,256]{1,0:T(8,128)}, f32[256,256]{1,0:T(...) custom-call(bf16[4,4,32,256]{3,2,1,0:T(8,128)(2,1)S(1)} %get-tuple-element.17.gf_in, f32[4,256,256]{2,1,0:T(8,128)S(1)} %bitcast.3, ...), custom_call_target="tpu_custom_call" | custom-call | tf_op jit(solution)/shard_map/pallas_call | solution.py:681
